TPU v7x, 32 devices: a whole 2x2x4 slice. The times are simulated.
32 devices in a mesh: dp: 8 (over y, x, core), tensor: 4 (over z).
Axes of the slice: x: 2, y: 2, z: 4, core: 2. Of those that a mesh axis runs over, the one named last changes fastest.
Arguments:
- activations: bfloat16 [4096, 4096], P('dp'), may hold values from -1000 to 1000
- norm_gain: bfloat16 [4096], replicated, may hold values from 0.5 to 1.5
- query_blocks: bfloat16 [128, 32, 4096], P('dp', None, 'tensor'), may hold values from -64 to 64
- query_scales: int32 [128, 1, 4096], P('dp', None, 'tensor'), may hold values from -9 to -5
- key_blocks: bfloat16 [128, 32, 512], P('dp', None, 'tensor'), may hold values from -64 to 64
- key_scales: int32 [128, 1, 512], P('dp', None, 'tensor'), may hold values from -9 to -5
- value_blocks: bfloat16 [128, 32, 512], P('dp', None, 'tensor'), may hold values from -6 to 6
- value_scales: int32 [128, 1, 512], P('dp', None, 'tensor'), may hold values from -9 to -5
- output_blocks: bfloat16 [128, 32, 4096], P('tensor', None, 'dp'), may hold values from -6 to 6
- output_scales: int32 [128, 1, 4096], P('tensor', None, 'dp'), may hold values from -9 to -5
Outputs:
- attended: bfloat16 [4096, 4096], P('dp')
All inputs are finite; a program needn't handle non-finite values.
Results may differ from a plain program's by a relative error of at most 0.015.
The roundings to bfloat16 on the way count: a program that leaves them out, or rounds other values in their place, can miss the bound.
Values may be sent and summed in bfloat16 or wider, within the bound.
No kernel may reach another device: no remote copies, remote signals or barrier semaphores. Data moves between devices by JAX's collectives and lax.ppermute only.
A program may use at most 128 MiB of HBM per device.

v0:
```python
import math
import jax
import jax.numpy as jnp
from jax import lax
from jax.sharding import PartitionSpec as P

HEAD_DIM = 128
SEQ = 256
EPS = 1e-05
ROPE_BASE = 500000.0


def dequant(blocks, scales):
    factor = jnp.exp2(scales.astype(jnp.float32)).astype(blocks.dtype)
    weight = blocks * factor
    return weight.reshape(weight.shape[0] * weight.shape[1], weight.shape[2])


def rotate_pairs(states, positions):
    half_dim = states.shape[-1] // 2
    frequency = jnp.exp(
        -math.log(ROPE_BASE) * jnp.arange(half_dim, dtype=jnp.float32) * 2.0 / states.shape[-1]
    )
    angles = positions.astype(jnp.float32)[:, None] * frequency[None, :]
    cosine = jnp.cos(angles)[None, :, None, :]
    sine_part = jnp.sin(angles)[None, :, None, :]
    first = states[..., :half_dim]
    second = states[..., half_dim:]
    return jnp.concatenate(
        [first * cosine - second * sine_part, second * cosine + first * sine_part], axis=-1
    )


def attend(query_states, key_states, value_states, kv_count):
    tokens_here = query_states.shape[0]
    count = tokens_here // SEQ
    positions = jnp.arange(SEQ, dtype=jnp.int32)
    queries = rotate_pairs(query_states.reshape(count, SEQ, -1, HEAD_DIM), positions).astype(
        jnp.bfloat16
    )
    rotated_keys = rotate_pairs(
        key_states.reshape(count, SEQ, kv_count, HEAD_DIM), positions
    ).astype(jnp.bfloat16)
    value_heads = value_states.astype(jnp.bfloat16).reshape(count, SEQ, kv_count, HEAD_DIM)
    group_size = queries.shape[2] // kv_count
    queries = queries.reshape(count, SEQ, kv_count, group_size, HEAD_DIM)
    scores = jnp.einsum(
        "sqkgd,stkd->skgqt", queries, rotated_keys, preferred_element_type=jnp.float32
    ) * HEAD_DIM ** (-0.5)
    visible = positions[:, None] >= positions[None, :]
    scores = jnp.where(visible, scores, -jnp.inf)
    attn_weights = jax.nn.softmax(scores, axis=-1).astype(jnp.bfloat16)
    context = jnp.einsum(
        "skgqt,stkd->sqkgd", attn_weights, value_heads, preferred_element_type=jnp.float32
    )
    return context.astype(jnp.bfloat16).reshape(tokens_here, -1)


def shards(
    activations,
    norm_gain,
    query_blocks,
    query_scales,
    key_blocks,
    key_scales,
    value_blocks,
    value_scales,
    output_blocks,
    output_scales,
):
    query_exps = query_scales.astype(jnp.bfloat16)
    key_exps = key_scales.astype(jnp.bfloat16)
    value_exps = value_scales.astype(jnp.bfloat16)
    output_exps = output_scales.astype(jnp.bfloat16)
    wide_rows = activations.astype(jnp.float32)
    inverse = lax.rsqrt(jnp.mean(wide_rows * wide_rows, axis=-1, keepdims=True) + EPS)
    normed = (wide_rows * inverse * norm_gain.astype(jnp.float32)).astype(jnp.bfloat16)

    def product(blocks, scales):
        return jnp.dot(normed, dequant(blocks, scales), preferred_element_type=jnp.float32)

    def add_one(pieces):
        return product(pieces[0], pieces[1])

    query_states = add_one(
        (
            lax.all_gather(query_blocks, "dp", axis=0, tiled=True),
            lax.all_gather(query_exps, "dp", axis=0, tiled=True),
        )
    )
    key_states = add_one(
        (
            lax.all_gather(key_blocks, "dp", axis=0, tiled=True),
            lax.all_gather(key_exps, "dp", axis=0, tiled=True),
        )
    )
    value_states = add_one(
        (
            lax.all_gather(value_blocks, "dp", axis=0, tiled=True),
            lax.all_gather(value_exps, "dp", axis=0, tiled=True),
        )
    )
    context = attend(query_states, key_states, value_states, key_blocks.shape[2] // HEAD_DIM)
    pieces = (
        lax.all_gather(output_blocks, "dp", axis=2, tiled=True),
        lax.all_gather(output_exps, "dp", axis=2, tiled=True),
    )
    block_out = jnp.dot(context, dequant(pieces[0], pieces[1]), preferred_element_type=jnp.float32)
    return lax.psum(block_out.astype(jnp.bfloat16), "tensor")


def solution(mesh):
    placed = (
        P("dp", None),
        P(),
        P("dp", None, "tensor"),
        P("dp", None, "tensor"),
        P("dp", None, "tensor"),
        P("dp", None, "tensor"),
        P("dp", None, "tensor"),
        P("dp", None, "tensor"),
        P("tensor", None, "dp"),
        P("tensor", None, "dp"),
    )
    return jax.shard_map(
        shards, mesh=mesh, in_specs=placed, out_specs=P("dp", None), check_vma=False
    )
```

profile of v0, /device:TPU:0, one launch (start us, length us, event | category | flops | bytes accessed | tf_op | source)
XLA Modules:
  0.0 358.5 jit_solution(17838992438456256269)
XLA Ops:
  6.5 0.0 copy-start.1
  6.5 0.0 all-gather.7.cloned.1.call-start
  6.5 0.7 all-gather.7.cloned.1.call-update
  7.3 0.0 all-gather.5.cloned.1.call-start
  7.3 0.7 all-gather.5.cloned.1.call-update
  8.0 0.0 all-gather.9.cloned.1.call-start
  8.1 0.7 all-gather.9.cloned.1.call-update
  8.7 0.0 all-gather.11.cloned.1.call-start
  8.8 0.5 all-gather.11.cloned.1.call-update
  9.3 0.0 all-reduce.2.cloned.1.call-start
  9.4 0.0 copy-start
  9.4 0.9 convert_element_type.93
  10.2 0.9 convert_element_type.99
  11.1 0.7 convert_element_type.95
  11.8 0.9 convert_element_type.110
  12.7 12.4 %all_gather.31 = bf16[32,1,4096]{2,1,0:T(2,128)(2,1)S(1)} all-gather(bf16[32,1,512]{2,1,0:T(2,128)(2,1)S(1)} %convert_element_type.110), channel_id=1, replica_groups=mesh['dp'=8,'tensor'=4] {'dp'}, dimensions={2}, use_global_device_ids=true | all-gather | bytes 294912 | tf_op jit(solution)/shard_map/all_gather | solution.py:106
  25.1 0.9 exponential_convert_fusion
  26.1 0.3 copy.53
  26.4 9.1 %all_gather.27 = bf16[128,1,128]{2,0,1:T(8,128)(2,1)S(1)} all-gather(bf16[16,1,128]{2,0,1:T(8,128)(2,1)S(1)} %convert_element_type.99), channel_id=1, replica_groups=mesh['dp'=8,'tensor'=4] {'dp'}, dimensions={0}, use_global_device_ids=true | all-gather | bytes 36864 | tf_op jit(solution)/shard_map/all_gather | solution.py:94
  35.5 8.3 %all_gather.25 = bf16[128,1,128]{2,0,1:T(8,128)(2,1)S(1)} all-gather(bf16[16,1,128]{2,0,1:T(8,128)(2,1)S(1)} %convert_element_type.95), channel_id=1, replica_groups=mesh['dp'=8,'tensor'=4] {'dp'}, dimensions={0}, use_global_device_ids=true | all-gather | bytes 36864 | tf_op jit(solution)/shard_map/all_gather | solution.py:100
  43.8 0.0 copy-done.1
  43.8 9.4 %all_gather.29 = bf16[128,1,1024]{2,0,1:T(8,128)(2,1)S(1)} all-gather(bf16[16,1,1024]{2,0,1:T(8,128)(2,1)S(1)} %copy_convert_fusion), channel_id=1, replica_groups=mesh['dp'=8,'tensor'=4] {'dp'}, dimensions={0}, use_global_device_ids=true | all-gather | bytes 294912 | tf_op jit(solution)/shard_map/all_gather | solution.py:88
  53.2 3.1 fusion
  56.4 0.3 multiply_cosine_fusion
  56.7 0.1 fusion.20
  56.8 0.0 copy-done
  56.8 3.6 %fusion.2 = bf16[512,4096]{1,0:T(8,128)(2,1)} fusion(bf16[512,4096]{1,0:T(8,128)(2,1)S(1)} %copy-done, f32[4096]{0:T(1024)S(1)} %convert_element_type.93, f32[512]{0:T(512)S(1)} %add_rsqrt_fusion), kind=kLoop, calls=%fused_computation.4 | loop fusion | flops 8388608 | bytes 8407040 | tf_op jit(solution)/shard_map/convert_element_type | solution.py:77
  60.4 0.0 all-gather.7.cloned.1.call-done
  60.4 1.3 broadcast_multiply_fusion.2
  61.8 3.7 %convolution_bitcast_fusion = f32[2,256,1,128]{1,3,0,2:T(8,128)S(1)} fusion(bf16[2,256,4096]{2,1,0:T(8,128)(2,1)} %bitcast.88, bf16[4096,128,1]{1,0,2:T(8,128)(2,1)S(1)} %bitcast.92), kind=kOutput, calls=%fused_computation.18 | convolution fusion | flops 536870912 | bytes 5505024 | tf_op jit(solution)/shard_map/dot_general | solution.py:80
  65.5 0.0 all-gather.5.cloned.1.call-done
  65.5 1.3 broadcast_multiply_fusion.3
  66.8 3.4 convolution_convert_fusion.1
  70.3 47.6 %all-gather.9.cloned.1.call-done = bf16[128,32,1024]{2,1,0:T(8,128)(2,1)} async-done(((bf16[16,32,1024]{2,1,0:T(8,128)(2,1)}), bf16[128,32,1024]{2,1,0:T(8,128)(2,1)}) %all-gather.9.cloned.1.call-update) | async-done | bytes 8388624 | tf_op jit(solution)/shard_map/all_gather | solution.py:87
  117.9 7.2 %broadcast_multiply_fusion.1 = bf16[128,32,1024]{2,1,0:T(8,128)(2,1)} fusion(bf16[128,32,1024]{2,1,0:T(8,128)(2,1)} %all-gather.9.cloned.1.call-done, bf16[128,1024]{1,0:T(8,128)(2,1)S(1)} %fusion.20), kind=kLoop, calls=%fused_computation.10 | loop fusion | flops 4194304 | bytes 17039360 | tf_op jit(solution)/shard_map/mul | solution.py:15
  125.1 12.1 %copy.28 = bf16[1024,4096]{1,0:T(8,128)(2,1)} copy(bf16[1024,4096]{0,1:T(8,128)(2,1)} %bitcast.87) | data formatting | bytes 16777216 | tf_op jit(solution)/shard_map/dot_general | solution.py:80
  137.2 8.2 %fusion.30 = f32[2,256,8,128]{1,3,2,0:T(8,128)S(1)} fusion(bf16[2,256,4096,1]{2,1,3,0:T(8,128)(2,1)} %bitcast.89, bf16[8,128,4096,1]{2,1,0,3:T(8,128)(2,1)} %bitcast.91), kind=kOutput, calls=%fused_computation.55 | convolution fusion | flops 4294967296 | bytes 14680064 | tf_op jit(solution)/shard_map/dot_general | solution.py:80
  145.4 0.3 subtract_convert_fusion
  145.8 0.8 fusion.4
  146.6 0.9 fusion.3
  147.5 1.3 fusion.11
  148.8 0.8 copy.33
  149.5 26.0 %all-gather.11.cloned.1.call-done = bf16[32,32,4096]{2,1,0:T(8,128)(2,1)} async-done(((bf16[32,32,512]{2,1,0:T(8,128)(2,1)}), bf16[32,32,4096]{2,1,0:T(8,128)(2,1)}) %all-gather.11.cloned.1.call-update) | async-done | bytes 8388624 | tf_op jit(solution)/shard_map/all_gather | solution.py:105
  175.5 7.3 %broadcast_multiply_fusion = bf16[32,32,4096]{2,1,0:T(8,128)(2,1)} fusion(bf16[32,32,4096]{2,1,0:T(8,128)(2,1)} %all-gather.11.cloned.1.call-done, bf16[32,4096]{1,0:T(8,128)(2,1)S(1)} %bitcast.93), kind=kLoop, calls=%fused_computation.7 | loop fusion | flops 4194304 | bytes 17039360 | tf_op jit(solution)/shard_map/mul | solution.py:15
  182.8 9.4 %convolution_convert_fusion = bf16[512,4096]{1,0:T(8,128)(2,1)} fusion(bf16[1024,4096]{1,0:T(8,128)(2,1)} %bitcast.90, bf16[64,8,8,128]{3,2,1,0:T(8,128)(2,1)S(1)} %bitcast.94), kind=kOutput, calls=%fused_computation.5 | convolution fusion | flops 4297064448 | bytes 13631488 | tf_op jit(solution)/shard_map/dot_general | solution.py:108
  192.2 0.0 all-reduce.2.cloned.1.call-update
  192.2 155.1 %all-reduce.2.cloned.1.call-done = bf16[512,4096]{1,0:T(8,128)(2,1)} async-done(((bf16[512,4096]{1,0:T(8,128)(2,1)}), bf16[512,4096]{1,0:T(8,128)(2,1)}) %all-reduce.2.cloned.1.call-update) | async-done | bytes 4194320 | tf_op jit(solution)/shard_map/psum | solution.py:109
  347.3 4.7 %copy.55 = bf16[512,4096]{1,0:T(8,128)(2,1)} copy(bf16[512,4096]{1,0:T(8,128)(2,1)} %all-reduce.2.cloned.1.call-done) | data formatting | bytes 8388608
  (8 shorter events, 0.1 us)
Async XLA Ops:
  6.5 37.2 %copy-start.1 = (s32[16,1,1024]{2,1,0:T(1,128)S(1)}, s32[16,1,1024]{2,1,0:T(1,128)}, u32[]{:S(2)}) copy-start(s32[16,1,1024]{2,1,0:T(1,128)} %param.13) | copy-start | bytes 196612
  6.5 53.9 %all-gather.7.cloned.1.call-start = ((), (), s32[]{:S(2)}) async-start(), calls=%async_computation.1 | async-start | bytes 1179648 | tf_op jit(solution)/shard_map/all_gather | solution.py:93
  7.3 58.3 %all-gather.5.cloned.1.call-start = ((), (), s32[]{:S(2)}) async-start(), calls=%async_computation | async-start | bytes 1179648 | tf_op jit(solution)/shard_map/all_gather | solution.py:99
  8.0 109.9 %all-gather.9.cloned.1.call-start = ((), (), s32[]{:S(2)}) async-start(), calls=%async_computation.2 | async-start | bytes 9437184 | tf_op jit(solution)/shard_map/all_gather | solution.py:87
  8.7 166.8 %all-gather.11.cloned.1.call-start = ((), (), s32[]{:S(2)}) async-start(), calls=%async_computation.3 | async-start | bytes 9437184 | tf_op jit(solution)/shard_map/all_gather | solution.py:105
  9.3 338.0 %all-reduce.2.cloned.1.call-start = ((), (), s32[]{:S(2)}) async-start(), calls=%async_computation.4 | async-start | bytes 8388608 | tf_op jit(solution)/shard_map/psum | solution.py:109
  9.4 47.4 %copy-start = (bf16[512,4096]{1,0:T(8,128)(2,1)S(1)}, bf16[512,4096]{1,0:T(8,128)(2,1)}, u32[]{:S(2)}) copy-start(bf16[512,4096]{1,0:T(8,128)(2,1)} %param.10) | copy-start | bytes 12582916
Sparse Core Ops, SparseCore 0:
  9.2 26.8 all-gather.6
  38.0 23.6 all-gather.4
  63.6 54.2 all-gather.8
  119.6 55.8 all-gather.10
  192.3 154.9 all-reduce.1
where the time goes:
time: 359 us
  waiting for transfers between devices  231 us (64%)
  blocking collectives  39.2 us (11%)
  other arithmetic  29.8 us (8%)
  matrix products  26.9 us (7%)
  local copies, waits for them, and re-layouts  17.9 us (5%)
  between operations  13.3 us (4%)
    psum x1, waiting for transfers between devices, shards(): return lax.psum(block_out.astype(jnp.bfloat16), 'tensor')  155 us
    all_gather x1, waiting for transfers between devices, shards(): lax.all_gather(query_blocks, 'dp', axis=0, tiled=True)  47.6 us
    all_gather x1, waiting for transfers between devices, shards(): lax.all_gather(output_blocks, 'dp', axis=2, tiled=True)  26 us
    mul x7, other arithmetic, dequant(): weight = blocks * factor  17.3 us
    dot_general x3, matrix products, product(): jnp.dot(normed, dequant(blocks, scales), preferred_element_type=jnp.float32)  15.4 us
    all_gather x1, blocking collectives, shards(): lax.all_gather(output_exps, 'dp', axis=2, tiled=True)  12.4 us
    dot_general x1, local copies, waits for them, and re-layouts, product(): jnp.dot(normed, dequant(blocks, scales), preferred_element_type=jnp.float32)  12.1 us
    all_gather x1, blocking collectives, shards(): lax.all_gather(query_exps, 'dp', axis=0, tiled=True)  9.4 us
  transfers between devices with their start and end apart: 5, of which 3 were waited for; matrix products, arithmetic and copies ran while one was open for 15% of the time, Pallas kernels for 0%

commit v1 on v0

--- a/solution.py
+++ b/solution.py
@@ -8,6 +8,13 @@
 SEQ = 256
 EPS = 1e-05
 ROPE_BASE = 500000.0
+
+
+def swapped_in(x, axis, dim):
+    size = lax.axis_size(axis)
+    blocks = jnp.stack([x for _ in range(size)])
+    blocks = lax.all_to_all(blocks, axis, split_axis=0, concat_axis=0)
+    return jnp.concatenate(blocks, axis=dim)
 
 
 def dequant(blocks, scales):
@@ -102,7 +109,7 @@
     )
     context = attend(query_states, key_states, value_states, key_blocks.shape[2] // HEAD_DIM)
     pieces = (
-        lax.all_gather(output_blocks, "dp", axis=2, tiled=True),
+        swapped_in(output_blocks, "dp", 2),
         lax.all_gather(output_exps, "dp", axis=2, tiled=True),
     )
     block_out = jnp.dot(context, dequant(pieces[0], pieces[1]), preferred_element_type=jnp.float32)

time: 359 us -> 417 us (1.16)
  blocking collectives: 39.2 us -> 134 us
  waiting for transfers between devices: 231 us -> 159 us
  local copies, waits for them, and re-layouts: 17.9 us -> 50.1 us
  starting transfers between devices: 0.15 us -> 5.46 us
    all_gather x1, blocking collectives: 12.4 us -> 106 us  [shards(): lax.all_gather(output_exps, 'dp', axis=2, tiled=True)]
    all_gather x1, waiting for transfers between devices: 47.6 us -> 0.01 us  [shards(): lax.all_gather(query_blocks, 'dp', axis=0, tiled=True)]
    all_gather x1 -> x0, waiting for transfers between devices: 26 us -> none  [shards(): lax.all_gather(output_blocks, 'dp', axis=2, tiled=True)]
    mul x0 -> x2, local copies, waits for them, and re-layouts: none -> 15.6 us  [dequant(): weight = blocks * factor]
    unnamed x6 -> x14, local copies, waits for them, and re-layouts: 5 us -> 16.9 us
    another operation x0 -> x1, local copies, waits for them, and re-layouts: none -> 5.53 us  [swapped_in(): blocks = jnp.stack([x for _ in range(size)])]
    all_to_all x0 -> x1, starting transfers between devices: none -> 5.34 us  [swapped_in(): blocks = lax.all_to_all(blocks, axis, split_axis=0, concat_axis=0)]
  transfers between devices with their start and end apart: 5 -> 5, of which waited for: 3 -> 1; matrix products, arithmetic and copies ran while one was open for 15% -> 14% of each run, Pallas kernels for 0% -> 0%
where the time goes in v1:
time: 417 us; the launch traced here: 416 us
  waiting for transfers between devices  159 us (38%)
  blocking collectives  134 us (32%)
  local copies, waits for them, and re-layouts  50.1 us (12%)
  other arithmetic  27.4 us (7%)
  matrix products  26.9 us (6%)
  between operations  13.4 us (3%)
  starting transfers between devices  5.46 us (1%)
    psum x1, waiting for transfers between devices, shards(): return lax.psum(block_out.astype(jnp.bfloat16), 'tensor')  157 us
    all_gather x1, blocking collectives, shards(): lax.all_gather(output_exps, 'dp', axis=2, tiled=True)  106 us
    mul x7, other arithmetic, dequant(): weight = blocks * factor  17.2 us
    unnamed x14, local copies, waits for them, and re-layouts  16.9 us
    mul x2, local copies, waits for them, and re-layouts, dequant(): weight = blocks * factor  15.6 us
    dot_general x3, matrix products, product(): jnp.dot(normed, dequant(blocks, scales), preferred_element_type=jnp.float32)  15.4 us
    dot_general x1, local copies, waits for them, and re-layouts, product(): jnp.dot(normed, dequant(blocks, scales), preferred_element_type=jnp.float32)  11.3 us
    all_gather x1, blocking collectives, shards(): lax.all_gather(query_exps, 'dp', axis=0, tiled=True)  9.97 us
  transfers between devices with their start and end apart: 5, of which 1 were waited for; matrix products, arithmetic and copies ran while one was open for 14% of the time, Pallas kernels for 0%

profile of v1, /device:TPU:0, one launch (start us, length us, event | category | flops | bytes accessed | tf_op | source)
XLA Modules:
  0.0 416.1 jit_solution(4603112732686308012)
XLA Ops:
  6.5 0.0 all-gather.6.cloned.1.call-start
  6.5 0.7 all-gather.6.cloned.1.call-update
  7.3 0.0 all-gather.4.cloned.1.call-start
  7.3 0.7 all-gather.4.cloned.1.call-update
  8.0 0.0 all-gather.8.cloned.1.call-start
  8.1 0.7 all-gather.8.cloned.1.call-update
  8.7 5.5 %stack.2 = bf16[8,32,32,512]{3,2,1,0:T(8,128)(2,1)} broadcast(bf16[32,32,512]{2,1,0:T(8,128)(2,1)} %param.18), dimensions={1,2,3} | broadcast | bytes 9437184 | tf_op jit(solution)/shard_map/stack | solution.py:15
  14.3 0.0 copy-start.4
  14.3 0.0 copy-start.1
  14.3 5.3 %all-to-all-start = ((bf16[8,32,32,512]{3,2,1,0:T(8,128)(2,1)}), bf16[8,32,32,512]{3,2,1,0:T(8,128)(2,1)}, u32[]{:S(2)}, u32[]{:S(2)}) async-start(bf16[8,32,32,512]{3,2,1,0:T(8,128)(2,1)} %stack.2), calls=%async_computation | async-start | bytes 16777216 | tf_op jit(solution)/shard_map/all_to_all | solution.py:16
  19.6 0.0 all-reduce.2.cloned.1.call-start
  19.7 0.0 copy-start
  19.7 0.0 copy-done.4
  19.7 0.0 copy-done.5
  19.7 0.0 copy-done.3
  19.8 0.0 copy-done.2
  19.8 106.0 %all_gather.27 = bf16[32,1,4096]{2,1,0:T(2,128)(2,1)S(1)} all-gather(bf16[32,1,512]{2,1,0:T(2,128)(2,1)S(1)} %convert_element_type.110), channel_id=1, replica_groups=mesh['dp'=8,'tensor'=4] {'dp'}, dimensions={2}, use_global_device_ids=true | all-gather | bytes 294912 | tf_op jit(solution)/shard_map/all_gather | solution.py:113
  125.9 1.8 convert_reduce_fusion
  127.7 8.9 %all_gather.22 = bf16[128,1,128]{2,0,1:T(8,128)(2,1)S(1)} all-gather(bf16[16,1,128]{2,0,1:T(8,128)(2,1)S(1)} %convert_element_type.95), channel_id=1, replica_groups=mesh['dp'=8,'tensor'=4] {'dp'}, dimensions={0}, use_global_device_ids=true | all-gather | bytes 36864 | tf_op jit(solution)/shard_map/all_gather | solution.py:107
  136.6 8.7 %all_gather.24 = bf16[128,1,128]{2,0,1:T(8,128)(2,1)S(1)} all-gather(bf16[16,1,128]{2,0,1:T(8,128)(2,1)S(1)} %convert_element_type.99), channel_id=1, replica_groups=mesh['dp'=8,'tensor'=4] {'dp'}, dimensions={0}, use_global_device_ids=true | all-gather | bytes 36864 | tf_op jit(solution)/shard_map/all_gather | solution.py:101
  145.3 0.0 copy-done.1
  145.4 10.0 %all_gather.26 = bf16[128,1,1024]{2,0,1:T(8,128)(2,1)S(1)} all-gather(bf16[16,1,1024]{2,0,1:T(8,128)(2,1)S(1)} %copy_convert_fusion), channel_id=1, replica_groups=mesh['dp'=8,'tensor'=4] {'dp'}, dimensions={0}, use_global_device_ids=true | all-gather | bytes 294912 | tf_op jit(solution)/shard_map/all_gather | solution.py:95
  155.4 3.1 fusion
  158.5 0.3 multiply_cosine_fusion
  158.8 0.1 fusion.20
  158.9 0.0 copy-done
  158.9 3.6 fusion.2
  162.6 1.3 broadcast_multiply_fusion.1
  163.9 3.7 convolution_bitcast_fusion
  167.6 0.0 all-gather.4.cloned.1.call-done
  167.7 1.3 broadcast_multiply_fusion.2
  169.0 3.4 convolution_convert_fusion.1
  172.4 0.0 all-to-all-done
  172.4 7.2 %bitcast_multiply_fusion = bf16[32,32,8,512]{3,1,0,2:T(8,128)(2,1)} fusion(bf16[8,32,32,512]{3,2,1,0:T(8,128)(2,1)} %all-to-all-done, bf16[32,8,512]{2,0,1:T(8,128)(2,1)S(1)} %bitcast.99), kind=kLoop, calls=%fused_computation.5 | loop fusion | flops 4194304 | bytes 17039360 | tf_op jit(solution)/shard_map/mul | solution.py:22
  179.7 15.6 %copy.36 = bf16[32,32,8,512]{3,2,1,0:T(8,128)(2,1)} copy(bf16[32,32,8,512]{3,1,0,2:T(8,128)(2,1)} %bitcast_multiply_fusion) | data formatting | bytes 16777216 | tf_op jit(solution)/shard_map/mul | solution.py:22
  195.3 12.2 %copy.50 = bf16[128,8,8,512]{3,1,2,0:T(8,128)(2,1)} copy(bf16[128,8,8,512]{3,2,1,0:T(8,128)(2,1)} %bitcast.93) | data formatting | bytes 16777216
  207.5 7.2 %broadcast_multiply_fusion = bf16[128,32,1024]{2,1,0:T(8,128)(2,1)} fusion(bf16[128,32,1024]{2,1,0:T(8,128)(2,1)} %all-gather.8.cloned.1.call-done, bf16[128,1024]{1,0:T(8,128)(2,1)S(1)} %fusion.20), kind=kLoop, calls=%fused_computation.10 | loop fusion | flops 4194304 | bytes 17039360 | tf_op jit(solution)/shard_map/mul | solution.py:22
  214.7 11.3 %copy.29 = bf16[1024,4096]{1,0:T(8,128)(2,1)} copy(bf16[1024,4096]{0,1:T(8,128)(2,1)} %bitcast.92) | data formatting | bytes 16777216 | tf_op jit(solution)/shard_map/dot_general | solution.py:87
  226.0 8.2 %fusion.30 = f32[2,256,8,128]{1,3,2,0:T(8,128)S(1)} fusion(bf16[2,256,4096,1]{2,1,3,0:T(8,128)(2,1)} %bitcast.95, bf16[8,128,4096,1]{2,1,0,3:T(8,128)(2,1)} %bitcast.97), kind=kOutput, calls=%fused_computation.55 | convolution fusion | flops 4294967296 | bytes 14680064 | tf_op jit(solution)/shard_map/dot_general | solution.py:87
  234.2 0.3 subtract_convert_fusion
  234.6 0.8 fusion.4
  235.4 0.9 fusion.3
  236.3 1.3 fusion.11
  237.6 0.8 copy.34
  238.3 9.4 %convolution_convert_fusion = bf16[512,4096]{1,0:T(8,128)(2,1)} fusion(bf16[1024,4096]{1,0:T(8,128)(2,1)} %bitcast.96, bf16[64,8,8,128]{3,2,1,0:T(8,128)(2,1)S(1)} %bitcast.102), kind=kOutput, calls=%fused_computation.6 | convolution fusion | flops 4297064448 | bytes 13631488 | tf_op jit(solution)/shard_map/dot_general | solution.py:115
  247.8 0.0 all-reduce.2.cloned.1.call-update
  247.8 157.1 %all-reduce.2.cloned.1.call-done = bf16[512,4096]{1,0:T(8,128)(2,1)} async-done(((bf16[512,4096]{1,0:T(8,128)(2,1)}), bf16[512,4096]{1,0:T(8,128)(2,1)}) %all-reduce.2.cloned.1.call-update) | async-done | bytes 4194320 | tf_op jit(solution)/shard_map/psum | solution.py:116
  404.8 4.7 %copy.59 = bf16[512,4096]{1,0:T(8,128)(2,1)} copy(bf16[512,4096]{1,0:T(8,128)(2,1)} %all-reduce.2.cloned.1.call-done) | data formatting | bytes 8388608
  (18 shorter events, 0.2 us)
Async XLA Ops:
  6.5 156.0 %all-gather.6.cloned.1.call-start = ((), (), s32[]{:S(2)}) async-start(), calls=%async_computation.2 | async-start | bytes 1179648 | tf_op jit(solution)/shard_map/all_gather | solution.py:100
  7.3 160.4 %all-gather.4.cloned.1.call-start = ((), (), s32[]{:S(2)}) async-start(), calls=%async_computation.1 | async-start | bytes 1179648 | tf_op jit(solution)/shard_map/all_gather | solution.py:106
  8.0 199.5 %all-gather.8.cloned.1.call-start = ((), (), s32[]{:S(2)}) async-start(), calls=%async_computation.3 | async-start | bytes 9437184 | tf_op jit(solution)/shard_map/all_gather | solution.py:94
  14.3 5.4 %copy-start.4 = (s32[16,1,128]{2,1,0:T(1,128)S(1)}, s32[16,1,128]{2,1,0:T(1,128)}, u32[]{:S(2)}) copy-start(s32[16,1,128]{2,1,0:T(1,128)} %param.15) | copy-start | bytes 24580
  14.3 5.4 %copy-start.5 = (s32[16,1,128]{2,1,0:T(1,128)S(1)}, s32[16,1,128]{2,1,0:T(1,128)}, u32[]{:S(2)}) copy-start(s32[16,1,128]{2,1,0:T(1,128)} %param.17) | copy-start | bytes 24580
  14.3 5.5 %copy-start.3 = (bf16[4096]{0:T(1024)(128)(2,1)S(1)}, bf16[4096]{0:T(1024)(128)(2,1)}, u32[]{:S(2)}) copy-start(bf16[4096]{0:T(1024)(128)(2,1)} %param.11) | copy-start | bytes 24580
  14.3 5.5 %copy-start.2 = (s32[32,1,512]{2,1,0:T(1,128)S(1)}, s32[32,1,512]{2,1,0:T(1,128)}, u32[]{:S(2)}) copy-start(s32[32,1,512]{2,1,0:T(1,128)} %param.19) | copy-start | bytes 196612
  14.3 131.1 %copy-start.1 = (s32[16,1,1024]{2,1,0:T(1,128)S(1)}, s32[16,1,1024]{2,1,0:T(1,128)}, u32[]{:S(2)}) copy-start(s32[16,1,1024]{2,1,0:T(1,128)} %param.13) | copy-start | bytes 196612
  14.3 158.1 %all-to-all-start = ((bf16[8,32,32,512]{3,2,1,0:T(8,128)(2,1)}), bf16[8,32,32,512]{3,2,1,0:T(8,128)(2,1)}, u32[]{:S(2)}, u32[]{:S(2)}) async-start(bf16[8,32,32,512]{3,2,1,0:T(8,128)(2,1)} %stack.2), calls=%async_computation | async-start | bytes 16777216 | tf_op jit(solution)/shard_map/all_to_all | solution.py:16
  19.6 385.2 %all-reduce.2.cloned.1.call-start = ((), (), s32[]{:S(2)}) async-start(), calls=%async_computation.4 | async-start | bytes 8388608 | tf_op jit(solution)/shard_map/psum | solution.py:116
  19.7 139.3 %copy-start = (bf16[512,4096]{1,0:T(8,128)(2,1)S(1)}, bf16[512,4096]{1,0:T(8,128)(2,1)}, u32[]{:S(2)}) copy-start(bf16[512,4096]{1,0:T(8,128)(2,1)} %param.10) | copy-start | bytes 12582916
Sparse Core Ops, SparseCore 0:
  9.2 67.1 all-gather.5
  78.3 34.8 all-gather.3
  115.1 54.9 all-gather.7
  247.9 156.8 all-reduce.1
